TPU v7x, 128 devices: a whole 4x4x4 slice. The times are simulated.
128 devices in a mesh: region: 64 (over z, y, x_hi, core), sub: 2 (over x_lo).
Axes of the slice: x: 4 (x_hi: 2, x_lo: 2; x = x_hi * 2 + x_lo), y: 4, z: 4, core: 2. Of those that a mesh axis runs over, the one named last changes fastest.
Arguments:
- sources: bfloat16 [128, 2048, 1280], P(('region', 'sub')), may hold values from -6 to 6
- coupling: bfloat16 [128, 2048, 2048], P(('region', 'sub')), may hold values from -0.0625 to 0.0625
- self_term: float32 [128, 2048], P(('region', 'sub')), may hold values from 0.25 to 1
- history: float32 [128, 4, 8, 640], P(('region', 'sub')), may hold values from -6 to 6
- line_nodes: int32 [128, 4, 8], P(('region', 'sub')), may hold values from -1 to 2047, as said below
- line_admit: float32 [128, 4, 8], P(('region', 'sub')), may hold values from 0 to 1, as said below
- term_region: int32 [32768, 1], P(('region', 'sub')), may hold values from 0 to 63; in each aligned block of 256 rows (0 to 255, 256 to 511, ...) at most 8 rows name the same one
- old_samples: bfloat16 [32768, 1280], P(('region', 'sub')), may hold values from -6 to 6
- prior_phasor: float32 [32768, 2, 128], P(('region', 'sub')), may hold values from -6 to 6
Outputs:
- next_history: float32 [128, 4, 8, 640], P(('region', 'sub'))
- node_voltages: bfloat16 [128, 2048, 1280], P(('region', 'sub'))
- phasors: float32 [65536, 2, 2, 128], P(('region', 'sub'))
Inputs may be any that keep to these rules, and one draw needn't show every extreme that they name: line_nodes[a, d, k] is -1 for an empty slot and for every slot of a direction with no subsystem; each subsystem has lines to each of its up to 4 neighbours in the directions of the steps, 1 to 8 lines a pair, in the first slots; [a, d, k] and the slot k of the opposite direction at the neighbour are both -1 or are the two ends of one line; some pair uses all 8 slots. line_admit is equal at the two ends of a line; it is 0 exactly where line_nodes is -1, else 0.25 or more. `term_region`: among the 256 terminals of one subsystem at most 8 name the same region, and in every draw some region is named by exactly 8 of one subsystem's terminals.
All inputs are finite; a program needn't handle non-finite values.
Results may differ from a plain program's by a relative error of at most 0.003.
Values sent between devices are 32-bit elements; how exact they have to be, the bound alone decides.
A program may use at most 128 MiB of HBM per device.

v0:
```python
import math

import jax
import jax.numpy as jnp
from jax import lax
from jax.sharding import PartitionSpec as P

NODES = 2048
NEIGH = 4
LPP = 8
DELAY = 40
SPANS = 2
SCEN = 16
TERM_DEV = 256
BINS = 8
DFT_LEN = 2048


def shifted(shard, axis, by):
    length = lax.axis_size(axis)
    pairs = [(i, i + by) for i in range(length) if 0 <= i + by < length]
    return lax.ppermute(shard, axis, pairs)


def fit_table():
    step_index = jnp.arange(SPANS * DELAY, dtype=jnp.int32)
    harmonic = jnp.arange(1, BINS + 1, dtype=jnp.int32)
    product = step_index[:, None] * harmonic[None, :] % DFT_LEN
    angles = product.astype(jnp.float32) * (2.0 * math.pi / DFT_LEN)
    norm_scale = 1.0 / math.sqrt(DFT_LEN)
    twiddle = jnp.stack([jnp.cos(angles), -jnp.sin(angles)], axis=1) * norm_scale
    span_ends = (jnp.arange(SPANS, dtype=jnp.int32) + 1) * DELAY
    reached = (step_index[:, None] < span_ends[None, :]).astype(jnp.float32)
    same_scen = jnp.eye(SCEN, dtype=jnp.float32)
    table = jnp.einsum("uj,uch,st->usjcht", reached, twiddle, same_scen)
    return table.reshape(SPANS * DELAY * SCEN, SPANS * 2 * BINS * SCEN)


def phasor_fit(differences, prior):
    row_count = differences.shape[0]
    running = jnp.dot(
        differences,
        fit_table(),
        precision=lax.Precision.HIGHEST,
        preferred_element_type=jnp.float32,
    )
    return running.reshape(row_count, SPANS, 2, BINS * SCEN) + prior[:, None]


def send_lines(outgoing):
    from_lower_sub = shifted(outgoing[1], "sub", 1)
    from_upper_sub = shifted(outgoing[0], "sub", -1)
    from_lower_region = shifted(outgoing[3], "region", 1)
    from_upper_region = shifted(outgoing[2], "region", -1)
    return jnp.stack([from_lower_sub, from_upper_sub, from_lower_region, from_upper_region], axis=0)


def body(
    sources,
    coupling,
    self_term,
    history,
    line_nodes,
    line_admit,
    term_region,
    old_samples,
    prior_phasor,
):
    source_block = sources[0]
    matrix = coupling[0]
    self_gain = self_term[0][:, None]
    incoming = history[0]
    span_cols = DELAY * SCEN
    end_nodes = line_nodes[0].reshape(-1)
    admit_col = line_admit[0].reshape(-1, 1)
    live_slot = end_nodes >= 0
    target_rows = jnp.where(live_slot, end_nodes, NODES)
    pick_rows = jnp.where(live_slot, end_nodes, 0)
    pieces = []
    node_pieces = []
    for span_index in range(SPANS):
        low = span_index * span_cols
        span_src = source_block[:, low : low + span_cols]
        line_rows = incoming.reshape(NEIGH * LPP, span_cols)
        injection = (
            jnp.zeros((NODES, span_cols), jnp.float32)
            .at[target_rows]
            .add(line_rows, mode="drop")
            .astype(jnp.bfloat16)
        )
        source_part = jnp.dot(matrix, span_src, preferred_element_type=jnp.float32)
        voltages = source_part + jnp.dot(matrix, injection, preferred_element_type=jnp.float32)
        voltages = voltages + self_gain * (
            span_src.astype(jnp.float32) + injection.astype(jnp.float32)
        )
        pieces.append(voltages[:TERM_DEV])
        node_pieces.append(voltages.astype(jnp.bfloat16))
        line_volts = voltages[pick_rows]
        outgoing = jnp.where(live_slot[:, None], 2.0 * admit_col * line_volts - line_rows, 0.0)
        incoming = send_lines(outgoing.reshape(NEIGH, LPP, span_cols))
    next_history = incoming[None]
    node_voltages = jnp.concatenate(node_pieces, axis=1)[None]
    waveforms = jnp.concatenate(pieces, axis=1)
    differences = waveforms - old_samples.astype(jnp.float32)
    region_count = lax.axis_size("region")
    capacity = max(2, 2 * TERM_DEV // region_count)
    regions = term_region[:, 0]
    onehot = (regions[:, None] == jnp.arange(region_count, dtype=jnp.int32)[None, :]).astype(
        jnp.int32
    )
    rank_in = jnp.cumsum(onehot, axis=0) - onehot
    slot_index = jnp.sum(rank_in * onehot, axis=1)
    dest_row = regions * capacity + slot_index
    slot_ids = jnp.arange(region_count * capacity, dtype=jnp.int32)
    pack_table = (slot_ids[:, None] == dest_row[None, :]).astype(jnp.float32)

    def pack_rows(values):
        flat = values.reshape(values.shape[0], -1)
        packed = jnp.dot(
            pack_table, flat, precision=lax.Precision.HIGHEST, preferred_element_type=jnp.float32
        )
        return packed.reshape((region_count, capacity) + values.shape[1:])

    item_waves = lax.all_to_all(
        pack_rows(differences), "region", split_axis=0, concat_axis=0, tiled=True
    )
    item_prior = lax.all_to_all(
        pack_rows(prior_phasor), "region", split_axis=0, concat_axis=0, tiled=True
    )
    lead_count = item_waves.shape[0]
    item_count = item_waves.shape[1]
    fitted = phasor_fit(
        item_waves.reshape(lead_count * item_count, -1),
        item_prior.reshape(lead_count * item_count, 2, -1),
    )
    result = fitted.reshape(lead_count, item_count, SPANS, 2, BINS * SCEN)
    phasors = result.reshape(region_count * capacity, SPANS, 2, BINS * SCEN)
    return (next_history, node_voltages, phasors)


def solution(mesh):
    return jax.shard_map(
        body,
        mesh=mesh,
        in_specs=(
            P(("region", "sub"), None, None),
            P(("region", "sub"), None, None),
            P(("region", "sub"), None),
            P(("region", "sub"), None, None, None),
            P(("region", "sub"), None, None),
            P(("region", "sub"), None, None),
            P(("region", "sub"), None),
            P(("region", "sub"), None),
            P(("region", "sub"), None, None),
        ),
        out_specs=(
            P(("region", "sub"), None, None, None),
            P(("region", "sub"), None, None),
            P(("region", "sub"), None, None, None),
        ),
        check_vma=False,
    )
```

profile of v0, /device:TPU:31, one launch (start us, length us, event | category | flops | bytes accessed | tf_op | source)
XLA Modules:
  0.0 212.3 jit_solution(12751153286922865914)
XLA Ops:
  0.6 0.7 fusion.41
  1.3 0.6 reduce-window.6
  1.9 0.2 slice_reduce_fusion
  2.2 0.8 fusion.40
  3.0 0.7 multiply_add_fusion.1
  3.6 1.0 copy.57
  4.6 0.1 copy.44
  4.7 1.2 fusion.30
  6.0 11.4 %all-to-all-start.1 = ((f32[64,8,2,128]{3,1,2,0:T(8,128)}), f32[64,8,2,128]{3,1,2,0:T(8,128)S(1)}, u32[]{:S(2)}, u32[]{:S(2)}) async-start(f32[64,8,2,128]{3,1,2,0:T(8,128)} %fusion.30), calls=%async_computation.1 | async-start | bytes 1048576 | tf_op jit(solution)/shard_map/all_to_all | solution.py:127
  17.4 0.8 reshape_squeeze.7
  18.2 0.7 broadcast_compare_fusion
  18.8 0.1 ge.23
  18.9 0.7 broadcast_multiply_fusion.1
  19.6 0.1 mul.118
  19.7 3.8 %scatter_custom_fusion = f32[2048,640]{1,0:T(8,128)} fusion(s32[32]{0:T(128)S(1)} %get-tuple-element.23, f32[]{:T(128)} %constant.15.clone.1, f32[1,4,8,640]{3,2,1,0:T(8,128)} %param.12), kind=kCustom, calls=%fused_computation.25 | custom fusion | flops 20480 | bytes 5324804 | tf_op jit(solution)/shard_map/scatter-add | solution.py:88
  23.5 3.6 %copy.36 = bf16[2048,640]{0,1:T(8,128)(2,1)S(1)} copy(f32[2048,640]{1,0:T(8,128)} %scatter_custom_fusion) | data formatting | bytes 7864320 | tf_op jit(solution)/shard_map/scatter-add | solution.py:88
  27.1 7.9 %copy.35 = bf16[1,2048,1280]{1,2,0:T(8,128)(2,1)} copy(bf16[1,2048,1280]{2,1,0:T(8,128)(2,1)} %param.9) | data formatting | bytes 10485760 | tf_op args[0]
  35.0 11.3 %fusion.4 = f32[2048,640]{0,1:T(8,128)} fusion(bf16[1,2048,2048]{2,1,0:T(8,128)(2,1)} %param.10, bf16[2048,1280]{0,1:T(8,128)(2,1)} %bitcast.116), kind=kOutput, calls=%fused_computation.9 | convolution fusion | flops 5368709120 | bytes 16252928 | tf_op jit(solution)/shard_map/dot_general | solution.py:91
  46.3 12.3 %fusion.57 = (bf16[2048,640]{0,1:T(8,128)(2,1)}, f32[2048,640]{0,1:T(8,128)}) fusion(bf16[2048,640]{0,1:T(8,128)(2,1)S(1)} %copy.36, bf16[2048,1280]{0,1:T(8,128)(2,1)S(1)} %bitcast.119, f32[2048]{0:T(1024)S(1)} %bitcast.139, f32[2048,640]{0,1:T(8,128)} %fusion.4, bf16[1,2048,2048]{2,1,0:T(8,128)(2,1)} %param.10), kind=kOutput, calls=%fused_computation.92 | convolution fusion | flops 5377884160 | bytes 29368320 | tf_op jit(solution)/shard_map/dot_general | solution.py:92
  58.6 5.9 %copy.37 = f32[2048,640]{1,0:T(8,128)} copy(f32[2048,640]{0,1:T(8,128)} %get-tuple-element.27) | data formatting | bytes 10485760 | tf_op jit(solution)/shard_map/add | solution.py:93
  64.6 3.1 %gather_fusion = f32[32,640]{1,0:T(8,128)S(1)} fusion(f32[2048,640]{1,0:T(8,128)} %copy.37, s32[1024]{0:T(1024)S(1)} %pad_clamp_fusion), kind=kCustom, calls=%fused_computation | custom fusion | bytes 163968 | tf_op jit(solution)/shard_map/gather | solution.py:98
  67.7 0.1 fusion.37
  67.8 1.3 collective-permute-start
  69.1 2.3 %collective-permute-start.3 = (f32[8,640]{1,0:T(8,128)S(1)}, f32[8,640]{1,0:T(8,128)S(1)}, u32[]{:S(2)}, u32[]{:S(2)}) collective-permute-start(f32[8,640]{1,0:T(8,128)S(1)} %get-tuple-element.17), channel_id=1, source_target_pairs={{2,0},{4,2},{6,4},{8,6},{10,8},{12,10},{14,12},{16,14},{18,16},{20... | collective-permute-start | bytes 61448 | tf_op jit(solution)/shard_map/ppermute | solution.py:22
  71.5 7.8 %collective-permute-start.2 = (f32[8,640]{1,0:T(8,128)S(1)}, f32[8,640]{1,0:T(8,128)S(1)}, u32[]{:S(2)}, u32[]{:S(2)}) collective-permute-start(f32[8,640]{1,0:T(8,128)S(1)} %get-tuple-element.18), channel_id=1, source_target_pairs={{0,2},{2,4},{4,6},{6,8},{8,10},{10,12},{12,14},{14,16},{16,18},{18... | collective-permute-start | bytes 61448 | tf_op jit(solution)/shard_map/ppermute | solution.py:22
  79.2 4.2 %collective-permute-start.1 = (f32[8,640]{1,0:T(8,128)S(1)}, f32[8,640]{1,0:T(8,128)S(1)}, u32[]{:S(2)}, u32[]{:S(2)}) collective-permute-start(f32[8,640]{1,0:T(8,128)S(1)} %get-tuple-element.19), channel_id=1, source_target_pairs={{1,0},{3,2},{5,4},{7,6},{9,8},{11,10},{13,12},{15,14},{17,16},{19,... | collective-permute-start | bytes 61448 | tf_op jit(solution)/shard_map/ppermute | solution.py:22
  83.4 0.0 copy-start.3
  83.4 11.2 %fusion.6 = f32[2048,640]{0,1:T(8,128)} fusion(bf16[1,2048,2048]{2,1,0:T(8,128)(2,1)} %param.10, bf16[2048,1280]{0,1:T(8,128)(2,1)} %bitcast.117), kind=kOutput, calls=%fused_computation.11 | convolution fusion | flops 5368709120 | bytes 16252928 | tf_op jit(solution)/shard_map/dot_general | solution.py:91
  94.6 0.1 fusion.50
  94.8 1.1 slice.79
  95.9 0.2 copy.41
  96.2 0.0 collective-permute-done
  96.2 0.0 collective-permute-done.3
  96.2 0.0 collective-permute-done.2
  96.2 0.0 collective-permute-done.1
  96.2 3.4 %scatter_custom_fusion.1 = f32[2048,640]{1,0:T(8,128)} fusion(s32[32]{0:T(128)S(1)} %get-tuple-element.23, f32[]{:T(128)} %constant.15.clone.1, f32[1,8,640]{2,1,0:T(8,128)S(1)} %bitcast.126, f32[]{:T(128)} %constant.46, f32[1,8,640]{2,1,0:T(8,128)S(1)} %bitcast.128, f32[1,8,640]{2,1,0:T(8,128)S(1)} %bitcast.130, f32[1,8,640]{2,1,0:T(8,128)S(1)} %bitcast.124), kind=kCustom, calls=%fused_computation.23 | custom fusion | flops 81920 | bytes 5324808 | tf_op jit(solution)/shard_map/scatter-add | solution.py:88
  99.6 5.0 %copy.38 = bf16[2048,640]{0,1:T(8,128)(2,1)} copy(f32[2048,640]{1,0:T(8,128)} %scatter_custom_fusion.1) | data formatting | bytes 7864320 | tf_op jit(solution)/shard_map/scatter-add | solution.py:88
  104.6 13.4 %fusion.56 = (bf16[2048,640]{0,1:T(8,128)(2,1)}, f32[2048,640]{0,1:T(8,128)S(1)}) fusion(bf16[2048,640]{0,1:T(8,128)(2,1)} %copy.38, bf16[2048,1280]{0,1:T(8,128)(2,1)} %bitcast.118, f32[2048]{0:T(1024)S(1)} %bitcast.140, f32[2048,640]{0,1:T(8,128)} %fusion.6, bf16[1,2048,2048]{2,1,0:T(8,128)(2,1)} %param.10), kind=kOutput, calls=%fused_computation.91 | convolution fusion | flops 5377884160 | bytes 29368320 | tf_op jit(solution)/shard_map/dot_general | solution.py:92
  118.0 2.4 %copy-done = f32[2048,640]{0,1:T(8,128)} copy-done((f32[2048,640]{0,1:T(8,128)}, f32[2048,640]{0,1:T(8,128)S(1)}, u32[]{:S(2)}) %copy-start) | copy-done | bytes 5242904
  120.3 0.1 slice.80
  120.4 2.8 %convolution_bitcast_fusion = f32[64,8,1280]{2,1,0:T(8,128)} fusion(f32[256,640]{0,1:T(8,128)S(1)} %slice.80, f32[256,640]{0,1:T(8,128)S(1)} %slice.79, bf16[256,1280]{0,1:T(8,128)(2,1)S(1)} %copy.41, s32[256]{0:T(256)S(1)} %multiply_add_fusion.1), kind=kOutput, calls=%fused_computation.18 | convolution fusion | flops 2014380032 | bytes 4588544 | tf_op jit(solution)/shard_map/dot_general | solution.py:119
  123.2 9.8 %all-to-all-start = ((f32[64,8,1280]{2,1,0:T(8,128)}), f32[64,8,1280]{2,1,0:T(8,128)S(1)}, u32[]{:S(2)}, u32[]{:S(2)}) async-start(f32[64,8,1280]{2,1,0:T(8,128)} %convolution_bitcast_fusion), calls=%async_computation | async-start | bytes 5242880 | tf_op jit(solution)/shard_map/all_to_all | solution.py:124
  133.0 0.1 copy.42
  133.2 0.2 broadcast_multiply_fusion
  133.4 9.7 %multiply_bitcast_fusion = f32[80,16,2,2,8,16]{5,4,3,2,1,0:T(8,128)} fusion(f32[16,16]{1,0:T(8,128)S(1)} %fusion.43, f32[80,2,8,2]{2,1,3,0:T(2,128)S(1)} %broadcast_multiply_fusion), kind=kLoop, calls=%fused_computation.4 | loop fusion | flops 655360 | bytes 2632704 | tf_op jit(solution)/shard_map/uj,uch,st->usjcht/transpose | solution.py:35
  143.1 18.2 %reshape.260 = f32[1280,512]{1,0:T(8,128)} reshape(f32[80,16,2,2,8,16]{5,4,3,2,1,0:T(8,128)} %multiply_bitcast_fusion) | data formatting | bytes 5242880 | tf_op jit(solution)/shard_map/reshape | solution.py:36
  161.3 3.2 %copy.50 = f32[512,1280]{1,0:T(8,128)} copy(f32[512,1280]{0,1:T(8,128)} %bitcast.115) | data formatting | bytes 5242880 | tf_op jit(solution)/shard_map/dot_general | solution.py:41
  164.5 5.9 %copy.39 = f32[2048,640]{1,0:T(8,128)} copy(f32[2048,640]{0,1:T(8,128)} %copy-done) | data formatting | bytes 10485760 | tf_op jit(solution)/shard_map/add | solution.py:93
  170.4 3.1 %gather_fusion.1 = f32[32,640]{1,0:T(8,128)S(1)} fusion(f32[2048,640]{1,0:T(8,128)} %copy.39, s32[1024]{0:T(1024)S(1)} %pad_clamp_fusion), kind=kCustom, calls=%fused_computation.1 | custom fusion | bytes 163968 | tf_op jit(solution)/shard_map/gather | solution.py:98
  173.6 0.1 subtract_select_fusion
  173.7 1.3 collective-permute-start.4
  175.0 2.3 %collective-permute-start.7 = (f32[8,640]{1,0:T(8,128)S(1)}, f32[8,640]{1,0:T(8,128)S(1)}, u32[]{:S(2)}, u32[]{:S(2)}) collective-permute-start(f32[8,640]{1,0:T(8,128)S(1)} %get-tuple-element.13), channel_id=1, source_target_pairs={{2,0},{4,2},{6,4},{8,6},{10,8},{12,10},{14,12},{16,14},{18,16},{20... | collective-permute-start | bytes 61448 | tf_op jit(solution)/shard_map/ppermute | solution.py:22
  177.3 7.8 %collective-permute-start.6 = (f32[8,640]{1,0:T(8,128)S(1)}, f32[8,640]{1,0:T(8,128)S(1)}, u32[]{:S(2)}, u32[]{:S(2)}) collective-permute-start(f32[8,640]{1,0:T(8,128)S(1)} %get-tuple-element.14), channel_id=1, source_target_pairs={{0,2},{2,4},{4,6},{6,8},{8,10},{10,12},{12,14},{14,16},{16,18},{18... | collective-permute-start | bytes 61448 | tf_op jit(solution)/shard_map/ppermute | solution.py:22
  185.1 4.0 %collective-permute-start.5 = (f32[8,640]{1,0:T(8,128)S(1)}, f32[8,640]{1,0:T(8,128)S(1)}, u32[]{:S(2)}, u32[]{:S(2)}) collective-permute-start(f32[8,640]{1,0:T(8,128)S(1)} %get-tuple-element.15), channel_id=1, source_target_pairs={{1,0},{3,2},{5,4},{7,6},{9,8},{11,10},{13,12},{15,14},{17,16},{19,... | collective-permute-start | bytes 61448 | tf_op jit(solution)/shard_map/ppermute | solution.py:22
  189.0 5.7 %maximum_bitcast_fusion = bf16[1,2048,1280]{1,2,0:T(8,128)(2,1)} fusion(bf16[2048,640]{0,1:T(8,128)(2,1)} %get-tuple-element.24, bf16[2048,640]{0,1:T(8,128)(2,1)} %get-tuple-element.26), kind=kLoop, calls=%fused_computation.13 | loop fusion | flops 10485760 | bytes 10485760 | tf_op jit(solution)/shard_map/broadcast_in_dim | solution.py:102
  194.7 7.9 %copy.46 = bf16[1,2048,1280]{2,1,0:T(8,128)(2,1)} copy(bf16[1,2048,1280]{1,2,0:T(8,128)(2,1)} %maximum_bitcast_fusion) | data formatting | bytes 10485760
  202.6 0.0 collective-permute-done.4
  202.6 0.0 collective-permute-done.7
  202.6 0.0 collective-permute-done.6
  202.6 0.6 maximum_bitcast_fusion.2
  203.3 1.1 copy.56
  204.3 0.0 all-to-all-done
  204.4 6.1 %fusion.24 = f32[512,2,2,128]{3,0,2,1:T(8,128)S(1)} fusion(f32[2,2,128,1280]{3,2,1,0:T(8,128)} %bitcast.114, f32[64,8,1280]{2,1,0:T(8,128)S(1)} %all-to-all-done, f32[512,2,128]{2,0,1:T(8,128)S(1)} %bitcast.120), kind=kOutput, calls=%fused_computation.29 | convolution fusion | flops 4026793984 | bytes 6815744 | tf_op jit(solution)/shard_map/dot_general | solution.py:41
  210.5 1.8 copy.47
  (24 shorter events, 0.1 us)
Async XLA Ops:
  6.0 117.3 %all-to-all-start.1 = ((f32[64,8,2,128]{3,1,2,0:T(8,128)}), f32[64,8,2,128]{3,1,2,0:T(8,128)S(1)}, u32[]{:S(2)}, u32[]{:S(2)}) async-start(f32[64,8,2,128]{3,1,2,0:T(8,128)} %fusion.30), calls=%async_computation.1 | async-start | bytes 1048576 | tf_op jit(solution)/shard_map/all_to_all | solution.py:127
  35.0 11.3 %copy-start.1 = (bf16[1,2048,1280]{1,2,0:T(8,128)(2,1)S(1)}, bf16[1,2048,1280]{1,2,0:T(8,128)(2,1)}, u32[]{:S(2)}) copy-start(bf16[1,2048,1280]{1,2,0:T(8,128)(2,1)} %copy.35) | copy-start | bytes 15728644
  35.0 11.3 %copy-start.5 = (f32[1,2048]{1,0:T(1,128)S(1)}, f32[1,2048]{1,0:T(1,128)}, u32[]{:S(2)}) copy-start(f32[1,2048]{1,0:T(1,128)} %param.11) | copy-start | bytes 24580
  58.6 9.1 %copy-start.4 = (f32[1,4,8,640]{3,2,1,0:T(8,128)S(1)}, f32[1,4,8,640]{3,2,1,0:T(8,128)}, u32[]{:S(2)}) copy-start(f32[1,4,8,640]{3,2,1,0:T(8,128)} %param.12) | copy-start | bytes 245764
  67.8 28.3 %collective-permute-start = (f32[8,640]{1,0:T(8,128)S(1)}, f32[8,640]{1,0:T(8,128)S(1)}, u32[]{:S(2)}, u32[]{:S(2)}) collective-permute-start(f32[8,640]{1,0:T(8,128)S(1)} %get-tuple-element.16), channel_id=1, source_target_pairs={{0,1},{2,3},{4,5},{6,7},{8,9},{10,11},{12,13},{14,15},{16,17},{18,... | collective-permute-start | bytes 61448 | tf_op jit(solution)/shard_map/ppermute | solution.py:22
  69.1 27.1 %collective-permute-start.3 = (f32[8,640]{1,0:T(8,128)S(1)}, f32[8,640]{1,0:T(8,128)S(1)}, u32[]{:S(2)}, u32[]{:S(2)}) collective-permute-start(f32[8,640]{1,0:T(8,128)S(1)} %get-tuple-element.17), channel_id=1, source_target_pairs={{2,0},{4,2},{6,4},{8,6},{10,8},{12,10},{14,12},{16,14},{18,16},{20... | collective-permute-start | bytes 61448 | tf_op jit(solution)/shard_map/ppermute | solution.py:22
  71.5 24.7 %collective-permute-start.2 = (f32[8,640]{1,0:T(8,128)S(1)}, f32[8,640]{1,0:T(8,128)S(1)}, u32[]{:S(2)}, u32[]{:S(2)}) collective-permute-start(f32[8,640]{1,0:T(8,128)S(1)} %get-tuple-element.18), channel_id=1, source_target_pairs={{0,2},{2,4},{4,6},{6,8},{8,10},{10,12},{12,14},{14,16},{16,18},{18... | collective-permute-start | bytes 61448 | tf_op jit(solution)/shard_map/ppermute | solution.py:22
  79.2 17.0 %collective-permute-start.1 = (f32[8,640]{1,0:T(8,128)S(1)}, f32[8,640]{1,0:T(8,128)S(1)}, u32[]{:S(2)}, u32[]{:S(2)}) collective-permute-start(f32[8,640]{1,0:T(8,128)S(1)} %get-tuple-element.19), channel_id=1, source_target_pairs={{1,0},{3,2},{5,4},{7,6},{9,8},{11,10},{13,12},{15,14},{17,16},{19,... | collective-permute-start | bytes 61448 | tf_op jit(solution)/shard_map/ppermute | solution.py:22
  83.4 12.5 %copy-start.3 = (bf16[256,1280]{1,0:T(8,128)(2,1)S(1)}, bf16[256,1280]{1,0:T(8,128)(2,1)}, u32[]{:S(2)}) copy-start(bf16[256,1280]{1,0:T(8,128)(2,1)} %param.16) | copy-start | bytes 1966084
  118.0 2.4 %copy-start = (f32[2048,640]{0,1:T(8,128)}, f32[2048,640]{0,1:T(8,128)S(1)}, u32[]{:S(2)}) copy-start(f32[2048,640]{0,1:T(8,128)S(1)} %get-tuple-element.25) | copy-start | bytes 15728644
  123.2 19.9 %copy-start.2 = (f32[64,8,2,128]{3,1,2,0:T(8,128)}, f32[64,8,2,128]{3,1,2,0:T(8,128)S(1)}, u32[]{:S(2)}) copy-start(f32[64,8,2,128]{3,1,2,0:T(8,128)S(1)} %all-to-all-done.1) | copy-start | bytes 1572868
  123.2 81.1 %all-to-all-start = ((f32[64,8,1280]{2,1,0:T(8,128)}), f32[64,8,1280]{2,1,0:T(8,128)S(1)}, u32[]{:S(2)}, u32[]{:S(2)}) async-start(f32[64,8,1280]{2,1,0:T(8,128)} %convolution_bitcast_fusion), calls=%async_computation | async-start | bytes 5242880 | tf_op jit(solution)/shard_map/all_to_all | solution.py:124
  173.7 28.9 %collective-permute-start.4 = (f32[8,640]{1,0:T(8,128)S(1)}, f32[8,640]{1,0:T(8,128)S(1)}, u32[]{:S(2)}, u32[]{:S(2)}) collective-permute-start(f32[8,640]{1,0:T(8,128)S(1)} %get-tuple-element.12), channel_id=1, source_target_pairs={{0,1},{2,3},{4,5},{6,7},{8,9},{10,11},{12,13},{14,15},{16,17},{18,... | collective-permute-start | bytes 61448 | tf_op jit(solution)/shard_map/ppermute | solution.py:22
  175.0 27.6 %collective-permute-start.7 = (f32[8,640]{1,0:T(8,128)S(1)}, f32[8,640]{1,0:T(8,128)S(1)}, u32[]{:S(2)}, u32[]{:S(2)}) collective-permute-start(f32[8,640]{1,0:T(8,128)S(1)} %get-tuple-element.13), channel_id=1, source_target_pairs={{2,0},{4,2},{6,4},{8,6},{10,8},{12,10},{14,12},{16,14},{18,16},{20... | collective-permute-start | bytes 61448 | tf_op jit(solution)/shard_map/ppermute | solution.py:22
  177.3 25.3 %collective-permute-start.6 = (f32[8,640]{1,0:T(8,128)S(1)}, f32[8,640]{1,0:T(8,128)S(1)}, u32[]{:S(2)}, u32[]{:S(2)}) collective-permute-start(f32[8,640]{1,0:T(8,128)S(1)} %get-tuple-element.14), channel_id=1, source_target_pairs={{0,2},{2,4},{4,6},{6,8},{8,10},{10,12},{12,14},{14,16},{16,18},{18... | collective-permute-start | bytes 61448 | tf_op jit(solution)/shard_map/ppermute | solution.py:22
  185.1 17.6 %collective-permute-start.5 = (f32[8,640]{1,0:T(8,128)S(1)}, f32[8,640]{1,0:T(8,128)S(1)}, u32[]{:S(2)}, u32[]{:S(2)}) collective-permute-start(f32[8,640]{1,0:T(8,128)S(1)} %get-tuple-element.15), channel_id=1, source_target_pairs={{1,0},{3,2},{5,4},{7,6},{9,8},{11,10},{13,12},{15,14},{17,16},{19,... | collective-permute-start | bytes 61448 | tf_op jit(solution)/shard_map/ppermute | solution.py:22
where the time goes:
time: 214 us; the launch traced here: 212 us
  local copies, waits for them, and re-layouts  72.8 us (34%)
  matrix products  58.3 us (27%)
  starting transfers between devices  52.1 us (24%)
  other arithmetic  28 us (13%)
    ppermute x8, starting transfers between devices, shifted(): return lax.ppermute(shard, axis, pairs)  30.9 us
    dot_general x2, matrix products, body(): jnp.dot(matrix, injection, preferred_element_type=jnp.float32)  25.7 us
    dot_general x2, matrix products, body(): source_part = jnp.dot(matrix, span_src, preferred_element_type=jnp.float32)  22.5 us
    unnamed x17, local copies, waits for them, and re-layouts  21.1 us
    reshape x1, local copies, waits for them, and re-layouts, fit_table(): return table.reshape(SPANS * DELAY * SCEN, SPANS * 2 * BINS * SCEN)  18.2 us
    add x2, local copies, waits for them, and re-layouts, body(): voltages + self_gain * (span_src.astype(jnp.float32) + injection.astype(j...  11.8 us
    all_to_all x1, starting transfers between devices, body(): lax.all_to_all(pack_rows(prior_phasor), 'region', split_axis=0, concat_ax...  11.4 us
    all_to_all x1, starting transfers between devices, body(): lax.all_to_all(pack_rows(differences), 'region', split_axis=0, concat_axi...  9.79 us
  transfers between devices with their start and end apart: 10, of which 0 were waited for; matrix products, arithmetic and copies ran while one was open for 68% of the time, Pallas kernels for 0%

commit v1 on v0

v1 whole, which is shorter than its diff:
```python
import math

import jax
import jax.numpy as jnp
import numpy as np
from jax import lax
from jax.experimental import pallas as pl
from jax.experimental.pallas import tpu as pltpu
from jax.sharding import PartitionSpec as P

NODES = 2048
NEIGH = 4
LPP = 8
SLOTS = NEIGH * LPP
DELAY = 40
SPANS = 2
SCEN = 16
TERM = 256
BINS = 8
DFT_LEN = 2048
COLS = DELAY * SCEN
WIDE = SPANS * COLS
REGIONS = 64
CAP = 8
BOX = REGIONS * CAP
LANES = 128
HARM = BINS * SCEN
PAD = 128
BLOCK = 256
SPLIT = 512
EARLY = 3
MESH = pl.DeviceIdType.MESH
F32 = jnp.float32
BF16 = jnp.bfloat16


def fit_tables():
    step = np.arange(SPANS * DELAY)
    bins = np.arange(1, BINS + 1)
    angle = (step[:, None] * bins[None, :] % DFT_LEN) * (2.0 * math.pi / DFT_LEN)
    wave = np.stack([np.cos(angle), -np.sin(angle)], axis=1) / math.sqrt(DFT_LEN)
    table = np.einsum("uch,st->uscht", wave, np.eye(SCEN))
    table = table.reshape(SPANS, COLS, 2 * HARM).astype(np.float32)
    high = table.astype(BF16)
    low = (table - high.astype(np.float32)).astype(BF16)
    return np.stack([high, low], axis=1)


def dot(a, b):
    return jnp.dot(a, b, preferred_element_type=F32)


def two(x):
    high = x.astype(BF16)
    return high, (x - high.astype(F32)).astype(BF16)


def stack4(*blocks):
    zero = jnp.zeros((SLOTS, blocks[0].shape[1]), BF16)
    blocks = blocks + (zero,) * (4 - len(blocks))
    return jnp.concatenate(blocks, axis=0)


def iota(shape, axis):
    return lax.broadcasted_iota(jnp.int32, shape, axis)


def kernel(
    nodes_ref,
    admit_ref,
    src_hbm,
    mat_hbm,
    old_hbm,
    prior_hbm,
    table_hbm,
    hist_ref,
    self_ref,
    region_ref,
    volt_ref,
    phasor_ref,
    next_ref,
    mat,
    rhs,
    old,
    prior,
    table,
    gain,
    picked,
    gathered,
    fresh,
    outgo,
    arrived,
    packed,
    landed,
    mat_sem,
    load_sem,
    line_send,
    line_recv,
    item_send,
    item_recv,
    own_sem,
):
    region = lax.axis_index("region")
    sub = lax.axis_index("sub")
    barrier = pltpu.get_barrier_semaphore()
    other_sub = {"region": region, "sub": 1 - sub}
    below = {"region": lax.rem(region + REGIONS - 1, REGIONS), "sub": sub}
    above = {"region": lax.rem(region + 1, REGIONS), "sub": sub}

    loads = [
        pltpu.make_async_copy(
            src_hbm.at[:, pl.ds(j * COLS, COLS)], rhs.at[:, pl.ds(PAD + j * COLS, COLS)], load_sem.at[j]
        )
        for j in range(SPANS)
    ]
    loads.append(pltpu.make_async_copy(old_hbm, old, load_sem.at[2]))
    loads.append(pltpu.make_async_copy(prior_hbm, prior, load_sem.at[3]))
    loads.append(pltpu.make_async_copy(table_hbm, table, load_sem.at[4]))
    mat_loads = [
        pltpu.make_async_copy(
            mat_hbm.at[pl.ds(i * BLOCK, BLOCK)], mat.at[pl.ds(i * BLOCK, BLOCK)], mat_sem.at[i]
        )
        for i in range(NODES // BLOCK)
    ]
    loads[0].start()
    mat_loads[0].start()
    loads[2].start()
    loads[3].start()
    loads[4].start()
    for load in mat_loads[1:]:
        load.start()
    loads[1].start()

    def greet(i, _):
        pl.semaphore_signal(
            barrier, inc=1, device_id={"region": lax.rem(region + i, REGIONS), "sub": sub}, device_id_type=MESH
        )
        return 0

    lax.fori_loop(1, REGIONS, greet, 0)
    pl.semaphore_signal(barrier, inc=1, device_id=other_sub, device_id_type=MESH)

    node_row = jnp.full((1, LANES), -1, jnp.int32)
    node_col = jnp.full((SLOTS, 1), -1, jnp.int32)
    admit_col = jnp.zeros((SLOTS, 1), F32)
    lane_slot = iota((1, LANES), 1) % SLOTS
    slot_id = iota((SLOTS, 1), 0)
    for k in range(SLOTS):
        node = nodes_ref[k // LPP, k % LPP]
        node_row = jnp.where(lane_slot == k, node, node_row)
        node_col = jnp.where(slot_id == k, node, node_col)
        admit_col = jnp.where(slot_id == k, admit_ref[k // LPP, k % LPP], admit_col)
    live = node_col >= 0
    same = (node_col == node_row) & live
    lane = iota((SLOTS, LANES), 1)
    earlier = jnp.where(same & (lane < slot_id), 1.0, 0.0)
    first = (jnp.sum(earlier, axis=1, keepdims=True) == 0.0) & live
    merge = jnp.where(same & (lane < 3 * SLOTS), 1.0, 0.0).astype(BF16)
    twice_admit = 2.0 * admit_col

    def line_injection(rows):
        high = rows.astype(BF16)
        rest = rows - high.astype(F32)
        mid = rest.astype(BF16)
        low = (rest - mid.astype(F32)).astype(BF16)
        total = dot(merge, stack4(high, mid, low))
        return jnp.where(first, total, 0.0).astype(BF16)

    def mark(i, _):
        rows = pl.ds(pl.multiple_of(i * BLOCK, BLOCK), BLOCK)
        number = iota((BLOCK, LANES), 0) + i * BLOCK
        rhs[rows, pl.ds(0, PAD)] = jnp.where(number == node_row, 1.0, 0.0).astype(BF16)
        diag = iota((BLOCK, BLOCK), 0) == iota((BLOCK, BLOCK), 1)
        gains = jnp.sum(jnp.where(diag, self_ref[:, rows], 0.0), axis=1, keepdims=True)
        gain[rows, :] = jnp.broadcast_to(gains, (BLOCK, LANES))
        return 0

    lax.fori_loop(0, NODES // BLOCK, mark, 0)
    chosen = jnp.where(node_col == iota((SLOTS, NODES), 1), 1.0, 0.0)
    line_gain = jnp.sum(chosen * self_ref[...], axis=1, keepdims=True)
    picked[SLOTS:, :] = chosen.astype(BF16)
    line_rows = hist_ref[...]
    injected = line_injection(line_rows)

    region_row = region_ref[...]
    square = (TERM, TERM)
    diag = iota(square, 0) == iota(square, 1)
    region_col = jnp.sum(jnp.where(diag, region_row, 0), axis=1, keepdims=True)
    before = (region_col == region_row) & (iota(square, 0) < iota(square, 1))
    rank_row = jnp.sum(jnp.where(before, 1, 0), axis=0, keepdims=True)
    slot_row = region_row * CAP + rank_row
    place = jnp.where(iota((BOX, TERM), 0) == slot_row, 1.0, 0.0).astype(BF16)

    def spectrum(values, j):
        high, low = two(values)
        return dot(high, table[j, 0]) + (dot(low, table[j, 0]) + dot(high, table[j, 1]))

    def pack(values):
        high, low = two(values)
        return dot(place, high) + dot(place, low)

    def post(j, boxes):
        for c in range(2):
            packed[j, c] = boxes[:, c * HARM : (c + 1) * HARM]

    def item_copy(j, to):
        return pltpu.make_async_remote_copy(
            packed.at[j, :, pl.ds(pl.multiple_of(to * CAP, CAP), CAP), :],
            landed.at[j, :, pl.ds(pl.multiple_of(region * CAP, CAP), CAP), :],
            item_send.at[j],
            item_recv.at[j],
            device_id={"region": to, "sub": sub},
            device_id_type=MESH,
        )

    def own_copy(j):
        own = pl.ds(pl.multiple_of(region * CAP, CAP), CAP)
        return pltpu.make_async_copy(packed.at[j, :, own, :], landed.at[j, :, own, :], own_sem.at[j])

    def send_items(j):
        own_copy(j).start()

        def send(i, _):
            item_copy(j, lax.rem(region + i, REGIONS)).start()
            return 0

        lax.fori_loop(1, REGIONS, send, 0)

    def line_copies(j):
        copies = []
        for at, count, to, device in ((0, 2, 0, other_sub), (2, 1, 3, below), (3, 1, 2, above)):
            copies.append(
                pltpu.make_async_remote_copy(
                    outgo.at[j, pl.ds(at, count)],
                    arrived.at[j, pl.ds(to, count)],
                    line_send.at[j, at],
                    line_recv.at[j, to],
                    device_id=device,
                    device_id_type=MESH,
                )
            )
        return copies

    def put_lines(j, line_volts, rows):
        going = jnp.where(live, twice_admit * line_volts - rows, 0.0)
        outgo[j, 0] = going[LPP : 2 * LPP]
        outgo[j, 1] = going[:LPP]
        outgo[j, 2] = going[2 * LPP : 3 * LPP]
        outgo[j, 3] = going[3 * LPP :]

    head = pl.ds(0, TERM)
    span0 = pl.ds(PAD, COLS)
    span1 = pl.ds(PAD + COLS, COLS)
    term_gain = gain[head, :][:, :1]
    loads[0].wait()
    mat_loads[0].wait()
    part = dot(mat[head, :], rhs[:, pl.ds(0, PAD + COLS)])
    reach = part[:, :PAD] + term_gain * rhs[head, pl.ds(0, PAD)].astype(F32)
    reach_high, reach_low = two(reach)
    term_lane = iota((TERM, LANES), 1)
    reach_parts = jnp.where(
        (term_lane < SLOTS) | ((term_lane >= 2 * SLOTS) & (term_lane < 3 * SLOTS)),
        reach_high.astype(F32),
        jnp.where(term_lane < 2 * SLOTS, reach_low.astype(F32), 0.0),
    ).astype(BF16)
    volts = part[:, PAD:] + term_gain * rhs[head, span0].astype(F32)
    volts = volts + dot(reach_parts, stack4(injected, injected))
    volt_ref[head, pl.ds(0, COLS)] = volts.astype(BF16)
    for load in loads[2:]:
        load.wait()
    base = jnp.concatenate([prior[pl.ds(0, TERM, stride=2), :], prior[pl.ds(1, TERM, stride=2), :]], axis=1)
    fit = base + spectrum(volts - old[:, :COLS].astype(F32), 0)
    post(0, pack(fit))

    for load in mat_loads[1:]:
        load.wait()

    def pick(k, _):
        node = jnp.maximum(nodes_ref[k // LPP, k % LPP], 0)
        group = lax.div(node, 16) * 16
        rows = mat[pl.ds(group, 16), :].astype(F32)
        row = jnp.sum(jnp.where(iota((16, 1), 0) == node - group, rows, 0.0), axis=0, keepdims=True)
        gathered[pl.ds(k, 1), :] = row
        return 0

    lax.fori_loop(0, SLOTS, pick, 0, unroll=4)
    picked[:SLOTS, :] = gathered[...].astype(BF16)
    line_part = dot(picked[...], rhs[:, pl.ds(0, PAD + COLS)])
    line_reach = line_part[:SLOTS, :PAD] + line_gain * jnp.where(same, 1.0, 0.0)
    line_high, line_low = two(line_reach)
    line_parts = jnp.where(
        lane < SLOTS, line_high.astype(F32), jnp.where(lane < 2 * SLOTS, line_low.astype(F32), 0.0)
    ).astype(BF16)
    line_volts = line_part[:SLOTS, PAD:] + line_gain * line_part[SLOTS:, PAD:]
    line_volts = line_volts + dot(line_parts, stack4(injected, injected))
    put_lines(0, line_volts, line_rows)

    pl.semaphore_wait(barrier, REGIONS)
    lines0 = line_copies(0)
    for copy in lines0:
        copy.start()
    send_items(0)

    loads[1].wait()
    fresh[...] = dot(mat[head, :], rhs[:, span1]) + term_gain * rhs[head, span1].astype(F32)
    fit = fit + spectrum(fresh[...] - old[:, COLS:].astype(F32), 1)
    post(1, pack(fit))
    reach_box = dot(place, reach_parts).astype(BF16)
    line_part = dot(picked[...], rhs[:, span1])
    line_base = line_part[:SLOTS] + line_gain * line_part[SLOTS:]

    def inject(columns, rows32):
        block = stack4(rows32)

        def step(i, _):
            rows = pl.ds(pl.multiple_of(i * BLOCK, BLOCK), BLOCK)
            added = dot(rhs[rows, pl.ds(0, PAD)], block)
            rhs[rows, columns] = (rhs[rows, columns].astype(F32) + added).astype(BF16)
            return 0

        lax.fori_loop(0, NODES // BLOCK, step, 0)

    def advance(low, high, first_col, count):
        def step(i, _):
            rows = pl.ds(pl.multiple_of(i * BLOCK, BLOCK), BLOCK)
            columns = pl.ds(PAD + first_col, count)
            total = dot(mat[rows, :], rhs[:, columns])
            total = total + gain[rows, :][:, :1] * rhs[rows, columns].astype(F32)
            volt_ref[rows, pl.ds(first_col, count)] = total.astype(BF16)
            return 0

        lax.fori_loop(low, high, step, 0)

    inject(span0, injected)
    advance(1, 1 + EARLY, 0, SPLIT)

    for copy in lines0:
        copy.wait()
    line_rows = arrived[0].reshape(SLOTS, COLS)
    injected = line_injection(line_rows)
    shift_high, shift_low = two(dot(injected, table[1, 0]) + dot(injected, table[1, 1]))
    boxes = dot(reach_box, stack4(shift_high, shift_high, shift_low))
    for c in range(2):
        packed[1, c] = packed[1, c] + boxes[:, c * HARM : (c + 1) * HARM]
    both = stack4(injected, injected)
    put_lines(1, line_base + dot(line_parts, both), line_rows)
    volt_ref[head, pl.ds(COLS, COLS)] = (fresh[...] + dot(reach_parts, both)).astype(BF16)
    send_items(1)
    lines1 = line_copies(1)
    for copy in lines1:
        copy.start()

    advance(1 + EARLY, NODES // BLOCK, 0, SPLIT)
    inject(span1, injected)
    advance(1, NODES // BLOCK, SPLIT, WIDE - SPLIT)

    for copy in lines1:
        copy.wait()
    next_ref[...] = arrived[1]
    for j in range(SPANS):
        own_copy(j).wait()
        sent = packed.at[j, :, pl.ds(0, BOX - CAP), :]
        pltpu.make_async_copy(sent, sent, item_send.at[j]).wait()
        came = landed.at[j, :, pl.ds(0, BOX - CAP), :]
        pltpu.make_async_copy(came, came, item_recv.at[j]).wait()
        for c in range(2):
            phasor_ref[pl.ds(2 * j + c, BOX, stride=4), :] = landed[j, c]


def body(
    sources,
    coupling,
    self_term,
    history,
    line_nodes,
    line_admit,
    term_region,
    old_samples,
    prior_phasor,
):
    any_space = pl.BlockSpec(memory_space=pl.ANY)
    vmem = pl.BlockSpec(memory_space=pltpu.VMEM)
    smem = pl.BlockSpec(memory_space=pltpu.SMEM)
    volts, phasors, following = pl.pallas_call(
        kernel,
        out_shape=(
            jax.ShapeDtypeStruct((NODES, WIDE), BF16),
            jax.ShapeDtypeStruct((BOX * 2 * SPANS, HARM), F32),
            jax.ShapeDtypeStruct((NEIGH, LPP, COLS), F32),
        ),
        in_specs=[smem, smem] + [any_space] * 5 + [vmem] * 3,
        out_specs=(vmem, vmem, vmem),
        scratch_shapes=[
            pltpu.VMEM((NODES, NODES), BF16),
            pltpu.VMEM((NODES, PAD + WIDE), BF16),
            pltpu.VMEM((TERM, WIDE), BF16),
            pltpu.VMEM((2 * TERM, HARM), F32),
            pltpu.VMEM((SPANS, 2, COLS, 2 * HARM), BF16),
            pltpu.VMEM((NODES, LANES), F32),
            pltpu.VMEM((2 * SLOTS, NODES), BF16),
            pltpu.VMEM((SLOTS, NODES), F32),
            pltpu.VMEM((TERM, COLS), F32),
            pltpu.VMEM((SPANS, NEIGH, LPP, COLS), F32),
            pltpu.VMEM((SPANS, NEIGH, LPP, COLS), F32),
            pltpu.VMEM((SPANS, 2, BOX, HARM), F32),
            pltpu.VMEM((SPANS, 2, BOX, HARM), F32),
            pltpu.SemaphoreType.DMA((NODES // BLOCK,)),
            pltpu.SemaphoreType.DMA((5,)),
            pltpu.SemaphoreType.DMA((SPANS, NEIGH)),
            pltpu.SemaphoreType.DMA((SPANS, NEIGH)),
            pltpu.SemaphoreType.DMA((SPANS,)),
            pltpu.SemaphoreType.DMA((SPANS,)),
            pltpu.SemaphoreType.DMA((SPANS,)),
        ],
        compiler_params=pltpu.CompilerParams(
            collective_id=0, has_side_effects=True, vmem_limit_bytes=56 << 20
        ),
        name="transient",
    )(
        line_nodes[0],
        line_admit[0],
        sources[0],
        coupling[0],
        old_samples,
        prior_phasor.reshape(2 * TERM, HARM),
        jnp.asarray(fit_tables()),
        history.reshape(SLOTS, COLS),
        self_term,
        term_region.reshape(1, TERM),
    )
    return following[None], volts[None], phasors.reshape(BOX, SPANS, 2, HARM)


def solution(mesh):
    return jax.shard_map(
        body,
        mesh=mesh,
        in_specs=(
            P(("region", "sub"), None, None),
            P(("region", "sub"), None, None),
            P(("region", "sub"), None),
            P(("region", "sub"), None, None, None),
            P(("region", "sub"), None, None),
            P(("region", "sub"), None, None),
            P(("region", "sub"), None),
            P(("region", "sub"), None),
            P(("region", "sub"), None, None),
        ),
        out_specs=(
            P(("region", "sub"), None, None, None),
            P(("region", "sub"), None, None),
            P(("region", "sub"), None, None, None),
        ),
        check_vma=False,
    )
```

time: 214 us -> 43.9 us (0.21)
  the two profiles are of different devices: /device:TPU:31 before, /device:TPU:0 now
where the time goes in v1:
time: 43.9 us; the launch traced here: 43.8 us
  Pallas kernels  35.3 us (80%)
  local copies, waits for them, and re-layouts  7.77 us (18%)
  between operations  0.64 us (1%)
    pallas_call x1, Pallas kernels, body(): pl.pallas_call(kernel, out_shape=(jax.ShapeDtypeStruct((NODES, WIDE), BF1...  35.3 us
    unnamed x5, local copies, waits for them, and re-layouts  7.77 us

profile of v1, /device:TPU:0, one launch (start us, length us, event | category | flops | bytes accessed | tf_op | source)
XLA Modules:
  0.0 43.8 jit_solution(5491245505111797158)
XLA Ops:
  0.6 35.3 %transient.1 = (bf16[2048,1280]{1,0:T(8,128)(2,1)}, f32[2048,128]{1,0:T(8,128)}, f32[4,8,640]{2,1,0:T(8,128)}) custom-call(s32[4,8]{1,0:T(4,128)} %bitcast.17, f32[4,8]{1,0:T(4,128)} %bitcast.18, bf16[2048,1280]{1,0:T(8,128)(2,1)} %bitcast.11, bf16[2048,2048]{1,0:T(8,128)(2,1)} %bitcast.10, bf16[256,1280]{1,0:T(8,128)(2,1)} %old_hbm.1, f32[512,128]{1,0:T(8,128)} %bitcast.14, ...), custom_call_target="tpu_custom_call" | custom-call | tf_op jit(solution)/shard_map/transient/pallas_call | solution.py:384
  36.0 1.5 %copy.16 = f32[1,4,8,640]{3,2,1,0:T(8,128)} copy(f32[1,4,8,640]{3,2,1,0:T(8,128)} %bitcast.16) | data formatting | bytes 163840
  37.5 0.0 copy-start
  37.5 5.3 %copy.17 = bf16[1,2048,1280]{2,1,0:T(8,128)(2,1)} copy(bf16[1,2048,1280]{2,1,0:T(8,128)(2,1)} %bitcast.12) | data formatting | bytes 10485760
  42.8 0.0 copy-done
  42.8 1.0 %copy.18 = f32[512,2,2,128]{3,2,1,0:T(2,128)} copy(f32[512,2,2,128]{3,2,1,0:T(2,128)S(1)} %bitcast.13) | data formatting | bytes 2097152
Async XLA Ops:
  37.5 5.3 %copy-start = (f32[2048,128]{1,0:T(8,128)S(1)}, f32[2048,128]{1,0:T(8,128)}, u32[]{:S(2)}) copy-start(f32[2048,128]{1,0:T(8,128)} %get-tuple-element.8) | copy-start | bytes 3145732

commit v2 on v1

--- a/solution.py
+++ b/solution.py
@@ -27,11 +27,32 @@
 HARM = BINS * SCEN
 PAD = 128
 BLOCK = 256
-SPLIT = 512
-EARLY = 3
+LATE = 1
+PIECE = 8
+FILL = 512
+CHUNKS = 8
 MESH = pl.DeviceIdType.MESH
 F32 = jnp.float32
 BF16 = jnp.bfloat16
+HELD = (
+    ((NODES, WIDE), BF16),
+    ((SPANS, 2, BOX, HARM), F32),
+    ((SPANS, NEIGH, LPP, COLS), F32),
+    ((2 * SLOTS + NODES, NODES), BF16),
+    ((NODES, PAD + WIDE), BF16),
+    ((NODES, LANES), F32),
+)
+RESULTS = (
+    ((NODES, WIDE), BF16),
+    ((BOX * 2 * SPANS, HARM), F32),
+    ((NEIGH, LPP, COLS), F32),
+)
+
+
+def far_first():
+    away = (0, 1, 2, 1)
+    offsets = [(a, b, c, d) for a in range(4) for b in range(4) for c in range(2) for d in range(2)]
+    return sorted(offsets[1:], key=lambda o: -(away[o[0]] + away[o[1]] + 2 * o[2]))
 
 
 def fit_tables():
@@ -77,21 +98,18 @@
     self_ref,
     region_ref,
     volt_ref,
-    phasor_ref,
-    next_ref,
+    landed,
+    arrived,
     mat,
     rhs,
+    gain,
     old,
     prior,
     table,
-    gain,
-    picked,
-    gathered,
+    groups,
     fresh,
     outgo,
-    arrived,
     packed,
-    landed,
     mat_sem,
     load_sem,
     line_send,
@@ -115,29 +133,32 @@
     ]
     loads.append(pltpu.make_async_copy(old_hbm, old, load_sem.at[2]))
     loads.append(pltpu.make_async_copy(prior_hbm, prior, load_sem.at[3]))
-    loads.append(pltpu.make_async_copy(table_hbm, table, load_sem.at[4]))
+    for j in range(SPANS):
+        loads.append(pltpu.make_async_copy(table_hbm.at[j], table.at[j], load_sem.at[4 + j]))
     mat_loads = [
         pltpu.make_async_copy(
-            mat_hbm.at[pl.ds(i * BLOCK, BLOCK)], mat.at[pl.ds(i * BLOCK, BLOCK)], mat_sem.at[i]
+            mat_hbm.at[pl.ds(i * BLOCK, BLOCK)],
+            mat.at[pl.ds(2 * SLOTS + i * BLOCK, BLOCK)],
+            mat_sem.at[i],
         )
         for i in range(NODES // BLOCK)
     ]
     loads[0].start()
-    mat_loads[0].start()
-    loads[2].start()
-    loads[3].start()
-    loads[4].start()
-    for load in mat_loads[1:]:
+    for load in mat_loads:
         load.start()
-    loads[1].start()
-
-    def greet(i, _):
+    for i in (2, 3, 4, 1, 5):
+        loads[i].start()
+
+    z_at, y_at, x_at, core_at = region // 16, region // 4 % 4, region // 2 % 2, region % 2
+    z_part = [(z_at + i) % 4 * 16 for i in range(4)]
+    y_part = [(y_at + i) % 4 * 4 for i in range(4)]
+    x_part = [(x_at + i) % 2 * 2 for i in range(2)]
+    core_part = [(core_at + i) % 2 for i in range(2)]
+    peers = [z_part[a] + y_part[b] + (x_part[c] + core_part[d]) for a, b, c, d in far_first()]
+    for peer in peers:
         pl.semaphore_signal(
-            barrier, inc=1, device_id={"region": lax.rem(region + i, REGIONS), "sub": sub}, device_id_type=MESH
+            barrier, inc=1, device_id={"region": peer, "sub": sub}, device_id_type=MESH
         )
-        return 0
-
-    lax.fori_loop(1, REGIONS, greet, 0)
     pl.semaphore_signal(barrier, inc=1, device_id=other_sub, device_id_type=MESH)
 
     node_row = jnp.full((1, LANES), -1, jnp.int32)
@@ -170,15 +191,17 @@
         rows = pl.ds(pl.multiple_of(i * BLOCK, BLOCK), BLOCK)
         number = iota((BLOCK, LANES), 0) + i * BLOCK
         rhs[rows, pl.ds(0, PAD)] = jnp.where(number == node_row, 1.0, 0.0).astype(BF16)
+        return 0
+
+    def weigh(i, _):
+        rows = pl.ds(pl.multiple_of(i * BLOCK, BLOCK), BLOCK)
         diag = iota((BLOCK, BLOCK), 0) == iota((BLOCK, BLOCK), 1)
         gains = jnp.sum(jnp.where(diag, self_ref[:, rows], 0.0), axis=1, keepdims=True)
         gain[rows, :] = jnp.broadcast_to(gains, (BLOCK, LANES))
         return 0
 
     lax.fori_loop(0, NODES // BLOCK, mark, 0)
-    chosen = jnp.where(node_col == iota((SLOTS, NODES), 1), 1.0, 0.0)
-    line_gain = jnp.sum(chosen * self_ref[...], axis=1, keepdims=True)
-    picked[SLOTS:, :] = chosen.astype(BF16)
+    weigh(0, 0)
     line_rows = hist_ref[...]
     injected = line_injection(line_rows)
 
@@ -217,14 +240,9 @@
         own = pl.ds(pl.multiple_of(region * CAP, CAP), CAP)
         return pltpu.make_async_copy(packed.at[j, :, own, :], landed.at[j, :, own, :], own_sem.at[j])
 
-    def send_items(j):
-        own_copy(j).start()
-
-        def send(i, _):
-            item_copy(j, lax.rem(region + i, REGIONS)).start()
-            return 0
-
-        lax.fori_loop(1, REGIONS, send, 0)
+    def send_items(j, some):
+        for peer in some:
+            item_copy(j, peer).start()
 
     def line_copies(j):
         copies = []
@@ -254,7 +272,7 @@
     term_gain = gain[head, :][:, :1]
     loads[0].wait()
     mat_loads[0].wait()
-    part = dot(mat[head, :], rhs[:, pl.ds(0, PAD + COLS)])
+    part = dot(mat[pl.ds(2 * SLOTS, TERM), :], rhs[:, pl.ds(0, PAD + COLS)])
     reach = part[:, :PAD] + term_gain * rhs[head, pl.ds(0, PAD)].astype(F32)
     reach_high, reach_low = two(reach)
     term_lane = iota((TERM, LANES), 1)
@@ -264,28 +282,22 @@
         jnp.where(term_lane < 2 * SLOTS, reach_low.astype(F32), 0.0),
     ).astype(BF16)
     volts = part[:, PAD:] + term_gain * rhs[head, span0].astype(F32)
-    volts = volts + dot(reach_parts, stack4(injected, injected))
-    volt_ref[head, pl.ds(0, COLS)] = volts.astype(BF16)
-    for load in loads[2:]:
-        load.wait()
-    base = jnp.concatenate([prior[pl.ds(0, TERM, stride=2), :], prior[pl.ds(1, TERM, stride=2), :]], axis=1)
-    fit = base + spectrum(volts - old[:, :COLS].astype(F32), 0)
-    post(0, pack(fit))
-
+    fresh[0] = volts + dot(reach_parts, stack4(injected, injected))
+
+    lax.fori_loop(1, NODES // BLOCK, weigh, 0)
+    chosen = jnp.where(node_col == iota((SLOTS, NODES), 1), 1.0, 0.0)
+    line_gain = jnp.sum(chosen * self_ref[...], axis=1, keepdims=True)
+    mat[SLOTS : 2 * SLOTS, :] = chosen.astype(BF16)
+    node_at = jnp.maximum(node_col, 0) % PIECE + slot_id * PIECE
+    choice = jnp.where(iota((SLOTS, SLOTS * PIECE), 1) == node_at, 1.0, 0.0).astype(BF16)
     for load in mat_loads[1:]:
         load.wait()
-
-    def pick(k, _):
+    for k in range(SLOTS):
         node = jnp.maximum(nodes_ref[k // LPP, k % LPP], 0)
-        group = lax.div(node, 16) * 16
-        rows = mat[pl.ds(group, 16), :].astype(F32)
-        row = jnp.sum(jnp.where(iota((16, 1), 0) == node - group, rows, 0.0), axis=0, keepdims=True)
-        gathered[pl.ds(k, 1), :] = row
-        return 0
-
-    lax.fori_loop(0, SLOTS, pick, 0, unroll=4)
-    picked[:SLOTS, :] = gathered[...].astype(BF16)
-    line_part = dot(picked[...], rhs[:, pl.ds(0, PAD + COLS)])
+        group = 2 * SLOTS + lax.div(node, PIECE) * PIECE
+        groups[k * PIECE : (k + 1) * PIECE, :] = mat[pl.ds(group, PIECE), :]
+    mat[:SLOTS, :] = dot(choice, groups[...]).astype(BF16)
+    line_part = dot(mat[: 2 * SLOTS, :], rhs[:, pl.ds(0, PAD + COLS)])
     line_reach = line_part[:SLOTS, :PAD] + line_gain * jnp.where(same, 1.0, 0.0)
     line_high, line_low = two(line_reach)
     line_parts = jnp.where(
@@ -299,72 +311,104 @@
     lines0 = line_copies(0)
     for copy in lines0:
         copy.start()
-    send_items(0)
+
+    for load in loads[2:5]:
+        load.wait()
+    base = jnp.concatenate([prior[pl.ds(0, TERM, stride=2), :], prior[pl.ds(1, TERM, stride=2), :]], axis=1)
+    fit = base + spectrum(fresh[0] - old[:, :COLS].astype(F32), 0)
+    post(0, pack(fit))
+    send_items(0, peers)
+    own_copy(0).start()
+    volt_ref[head, pl.ds(0, COLS)] = fresh[0].astype(BF16)
 
     loads[1].wait()
-    fresh[...] = dot(mat[head, :], rhs[:, span1]) + term_gain * rhs[head, span1].astype(F32)
-    fit = fit + spectrum(fresh[...] - old[:, COLS:].astype(F32), 1)
+    loads[5].wait()
+    part = dot(mat[: 2 * SLOTS + TERM, :], rhs[:, span1])
+    line_base = part[:SLOTS] + line_gain * part[SLOTS : 2 * SLOTS]
+    fresh[1] = part[2 * SLOTS :] + term_gain * rhs[head, span1].astype(F32)
+    fit = fit + spectrum(fresh[1] - old[:, COLS:].astype(F32), 1)
     post(1, pack(fit))
     reach_box = dot(place, reach_parts).astype(BF16)
-    line_part = dot(picked[...], rhs[:, span1])
-    line_base = line_part[:SLOTS] + line_gain * line_part[SLOTS:]
-
-    def inject(columns, rows32):
-        block = stack4(rows32)
-
-        def step(i, _):
-            rows = pl.ds(pl.multiple_of(i * BLOCK, BLOCK), BLOCK)
-            added = dot(rhs[rows, pl.ds(0, PAD)], block)
-            rhs[rows, columns] = (rhs[rows, columns].astype(F32) + added).astype(BF16)
-            return 0
-
-        lax.fori_loop(0, NODES // BLOCK, step, 0)
-
-    def advance(low, high, first_col, count):
-        def step(i, _):
-            rows = pl.ds(pl.multiple_of(i * BLOCK, BLOCK), BLOCK)
-            columns = pl.ds(PAD + first_col, count)
-            total = dot(mat[rows, :], rhs[:, columns])
-            total = total + gain[rows, :][:, :1] * rhs[rows, columns].astype(F32)
-            volt_ref[rows, pl.ds(first_col, count)] = total.astype(BF16)
-            return 0
-
-        lax.fori_loop(low, high, step, 0)
-
-    inject(span0, injected)
-    advance(1, 1 + EARLY, 0, SPLIT)
 
     for copy in lines0:
         copy.wait()
     line_rows = arrived[0].reshape(SLOTS, COLS)
-    injected = line_injection(line_rows)
-    shift_high, shift_low = two(dot(injected, table[1, 0]) + dot(injected, table[1, 1]))
+    late = line_injection(line_rows)
+    shift_high, shift_low = two(dot(late, table[1, 0]) + dot(late, table[1, 1]))
     boxes = dot(reach_box, stack4(shift_high, shift_high, shift_low))
     for c in range(2):
         packed[1, c] = packed[1, c] + boxes[:, c * HARM : (c + 1) * HARM]
-    both = stack4(injected, injected)
+    send_items(1, peers)
+    own_copy(1).start()
+    both = stack4(late, late)
     put_lines(1, line_base + dot(line_parts, both), line_rows)
-    volt_ref[head, pl.ds(COLS, COLS)] = (fresh[...] + dot(reach_parts, both)).astype(BF16)
-    send_items(1)
+    volt_ref[head, pl.ds(COLS, COLS)] = (fresh[1] + dot(reach_parts, both)).astype(BF16)
     lines1 = line_copies(1)
     for copy in lines1:
         copy.start()
 
-    advance(1 + EARLY, NODES // BLOCK, 0, SPLIT)
-    inject(span1, injected)
-    advance(1, NODES // BLOCK, SPLIT, WIDE - SPLIT)
+    injection = stack4(jnp.concatenate([injected, late], axis=1))
+
+    def inject(i, _):
+        rows = pl.ds(pl.multiple_of(i * FILL, FILL), FILL)
+        columns = pl.ds(PAD, WIDE)
+        added = dot(rhs[rows, pl.ds(0, PAD)], injection)
+        rhs[rows, columns] = (rhs[rows, columns].astype(F32) + added).astype(BF16)
+        return 0
+
+    lax.fori_loop(0, NODES // FILL, inject, 0)
+
+    def advance(i, _):
+        rows = pl.ds(pl.multiple_of(i * BLOCK, BLOCK), BLOCK)
+        total = dot(mat[pl.ds(2 * SLOTS + i * BLOCK, BLOCK), :], rhs[:, pl.ds(PAD, WIDE)])
+        total = total + gain[rows, :][:, :1] * rhs[rows, pl.ds(PAD, WIDE)].astype(F32)
+        volt_ref[rows, :] = total.astype(BF16)
+        return 0
+
+    lax.fori_loop(1, NODES // BLOCK - LATE, advance, 0)
 
     for copy in lines1:
         copy.wait()
-    next_ref[...] = arrived[1]
     for j in range(SPANS):
         own_copy(j).wait()
         sent = packed.at[j, :, pl.ds(0, BOX - CAP), :]
         pltpu.make_async_copy(sent, sent, item_send.at[j]).wait()
         came = landed.at[j, :, pl.ds(0, BOX - CAP), :]
         pltpu.make_async_copy(came, came, item_recv.at[j]).wait()
+
+
+def release(
+    volt_ref, landed, arrived, mat, rhs, gain, volt_hbm, phasor_hbm, next_hbm, phasors, last, sem
+):
+    done = NODES - LATE * BLOCK
+    rows = done // CHUNKS
+    copies = [
+        pltpu.make_async_copy(
+            volt_ref.at[pl.ds(i * rows, rows)], volt_hbm.at[pl.ds(i * rows, rows)], sem.at[i]
+        )
+        for i in range(CHUNKS)
+    ]
+    copies.append(pltpu.make_async_copy(arrived.at[SPANS - 1], next_hbm, sem.at[CHUNKS]))
+    for copy in copies:
+        copy.start()
+    for j in range(SPANS):
         for c in range(2):
-            phasor_ref[pl.ds(2 * j + c, BOX, stride=4), :] = landed[j, c]
+            phasors[pl.ds(2 * j + c, BOX, stride=2 * SPANS), :] = landed[j, c]
+    copies.append(pltpu.make_async_copy(phasors, phasor_hbm, sem.at[CHUNKS + 1]))
+    copies[-1].start()
+    for i in range(LATE):
+        low = done + i * BLOCK
+        total = dot(mat[2 * SLOTS + low : 2 * SLOTS + low + BLOCK, :], rhs[:, PAD:])
+        total = total + gain[low : low + BLOCK, :][:, :1] * rhs[low : low + BLOCK, PAD:].astype(F32)
+        last[i * BLOCK : (i + 1) * BLOCK, :] = total.astype(BF16)
+        copies.append(
+            pltpu.make_async_copy(
+                last.at[pl.ds(i * BLOCK, BLOCK)], volt_hbm.at[pl.ds(low, BLOCK)], sem.at[CHUNKS + 2 + i]
+            )
+        )
+        copies[-1].start()
+    for copy in copies:
+        copy.wait()
 
 
 def body(
@@ -379,33 +423,24 @@
     prior_phasor,
 ):
     any_space = pl.BlockSpec(memory_space=pl.ANY)
+    hbm = pl.BlockSpec(memory_space=pltpu.HBM)
     vmem = pl.BlockSpec(memory_space=pltpu.VMEM)
     smem = pl.BlockSpec(memory_space=pltpu.SMEM)
-    volts, phasors, following = pl.pallas_call(
+    held = pl.pallas_call(
         kernel,
-        out_shape=(
-            jax.ShapeDtypeStruct((NODES, WIDE), BF16),
-            jax.ShapeDtypeStruct((BOX * 2 * SPANS, HARM), F32),
-            jax.ShapeDtypeStruct((NEIGH, LPP, COLS), F32),
-        ),
-        in_specs=[smem, smem] + [any_space] * 5 + [vmem] * 3,
-        out_specs=(vmem, vmem, vmem),
+        out_shape=tuple(pltpu.VMEM(shape, dtype) for shape, dtype in HELD),
+        in_specs=[smem, smem] + [hbm] * 5 + [vmem] * 3,
+        out_specs=(vmem,) * len(HELD),
         scratch_shapes=[
-            pltpu.VMEM((NODES, NODES), BF16),
-            pltpu.VMEM((NODES, PAD + WIDE), BF16),
             pltpu.VMEM((TERM, WIDE), BF16),
             pltpu.VMEM((2 * TERM, HARM), F32),
             pltpu.VMEM((SPANS, 2, COLS, 2 * HARM), BF16),
-            pltpu.VMEM((NODES, LANES), F32),
-            pltpu.VMEM((2 * SLOTS, NODES), BF16),
-            pltpu.VMEM((SLOTS, NODES), F32),
-            pltpu.VMEM((TERM, COLS), F32),
-            pltpu.VMEM((SPANS, NEIGH, LPP, COLS), F32),
+            pltpu.VMEM((SLOTS * PIECE, NODES), BF16),
+            pltpu.VMEM((SPANS, TERM, COLS), F32),
             pltpu.VMEM((SPANS, NEIGH, LPP, COLS), F32),
             pltpu.VMEM((SPANS, 2, BOX, HARM), F32),
-            pltpu.VMEM((SPANS, 2, BOX, HARM), F32),
             pltpu.SemaphoreType.DMA((NODES // BLOCK,)),
-            pltpu.SemaphoreType.DMA((5,)),
+            pltpu.SemaphoreType.DMA((6,)),
             pltpu.SemaphoreType.DMA((SPANS, NEIGH)),
             pltpu.SemaphoreType.DMA((SPANS, NEIGH)),
             pltpu.SemaphoreType.DMA((SPANS,)),
@@ -413,7 +448,7 @@
             pltpu.SemaphoreType.DMA((SPANS,)),
         ],
         compiler_params=pltpu.CompilerParams(
-            collective_id=0, has_side_effects=True, vmem_limit_bytes=56 << 20
+            collective_id=0, has_side_effects=True, vmem_limit_bytes=38 << 20
         ),
         name="transient",
     )(
@@ -428,6 +463,19 @@
         self_term,
         term_region.reshape(1, TERM),
     )
+    volts, phasors, following = pl.pallas_call(
+        release,
+        out_shape=tuple(jax.ShapeDtypeStruct(shape, dtype) for shape, dtype in RESULTS),
+        in_specs=[vmem] * len(HELD),
+        out_specs=(any_space,) * 3,
+        scratch_shapes=[
+            pltpu.VMEM((BOX * 2 * SPANS, HARM), F32),
+            pltpu.VMEM((LATE * BLOCK, WIDE), BF16),
+            pltpu.SemaphoreType.DMA((CHUNKS + 2 + LATE,)),
+        ],
+        compiler_params=pltpu.CompilerParams(vmem_limit_bytes=6 << 20),
+        name="release",
+    )(*held)
     return following[None], volts[None], phasors.reshape(BOX, SPANS, 2, HARM)
 
 

time: 43.9 us -> 34.6 us (0.79)
  local copies, waits for them, and re-layouts: 7.77 us -> 0 us
  Pallas kernels: 35.3 us -> 33.8 us
    unnamed x5 -> x0, local copies, waits for them, and re-layouts: 7.77 us -> none
    pallas_call x1 -> x2, Pallas kernels: 35.3 us -> 33.8 us  [the longest x1 31 us: body(): pl.pallas_call(kernel, out_shape=tuple((pltpu.VMEM(shape, dtype) for shap...]
where the time goes in v2:
time: 34.6 us; the launch traced here: 34.5 us
  Pallas kernels  33.8 us (98%)
  between operations  0.64 us (2%)
    pallas_call x1, Pallas kernels, body(): pl.pallas_call(kernel, out_shape=tuple((pltpu.VMEM(shape, dtype) for shap...  31 us
    pallas_call x1, Pallas kernels, body(): pl.pallas_call(release, out_shape=tuple((jax.ShapeDtypeStruct(shape, dtyp...  2.85 us

profile of v2, /device:TPU:0, one launch (start us, length us, event | category | flops | bytes accessed | tf_op | source)
XLA Modules:
  0.0 34.5 jit_solution(12669594190127360855)
XLA Ops:
  0.6 31.0 %transient.1 = (bf16[2048,1280]{1,0:T(8,128)(2,1)S(1)}, f32[2,2,512,128]{3,2,1,0:T(8,128)S(1)}, f32[2,4,8,640]{3,2,1,0:T(8,128)S(1)}, bf16[2112,2048]{1,0:T(8,12...) custom-call(s32[4,8]{1,0:T(4,128)} %bitcast.14, f32[4,8]{1,0:T(4,128)} %bitcast.15, ...), custom_call_target="tpu_custom_call" | custom-call | tf_op jit(solution)/shard_map/transient/pallas_call | solution.py:429
  31.6 2.8 %release.1 = (bf16[2048,1280]{1,0:T(8,128)(2,1)}, f32[2048,128]{1,0:T(8,128)}, f32[4,8,640]{2,1,0:T(8,128)}) custom-call(bf16[2048,1280]{1,0:T(8,128)(2,1)S(1)} %get-tuple-element.12.volt_ref, f32[2,2,512,128]{3,2,1,0:T(8,128)S(1)} %get-tuple-element.13.landed, f32[2,4,8,640]{3,2,1,0:T(8,128)S(1)} %get-tuple-element.14.arrived, ...), custom_call_target="tpu_custom_call" | custom-call | tf_op jit(solution)/shard_map/release/pallas_call | solution.py:466

commit v3 on v2

--- a/solution.py
+++ b/solution.py
@@ -29,7 +29,7 @@
 BLOCK = 256
 LATE = 1
 PIECE = 8
-FILL = 512
+FILL = 1024
 CHUNKS = 8
 MESH = pl.DeviceIdType.MESH
 F32 = jnp.float32
@@ -87,16 +87,16 @@
 
 
 def kernel(
-    nodes_ref,
-    admit_ref,
+    nodes_hbm,
+    admit_hbm,
     src_hbm,
     mat_hbm,
     old_hbm,
     prior_hbm,
     table_hbm,
-    hist_ref,
-    self_ref,
-    region_ref,
+    hist_hbm,
+    self_hbm,
+    region_hbm,
     volt_ref,
     landed,
     arrived,
@@ -117,6 +117,12 @@
     item_send,
     item_recv,
     own_sem,
+    nodes_ref,
+    admit_ref,
+    hist_ref,
+    self_ref,
+    region_ref,
+    small_sem,
 ):
     region = lax.axis_index("region")
     sub = lax.axis_index("sub")
@@ -131,10 +137,11 @@
         )
         for j in range(SPANS)
     ]
-    loads.append(pltpu.make_async_copy(old_hbm, old, load_sem.at[2]))
+    loads.append(pltpu.make_async_copy(old_hbm.at[:, :COLS], old.at[:, :COLS], load_sem.at[2]))
     loads.append(pltpu.make_async_copy(prior_hbm, prior, load_sem.at[3]))
     for j in range(SPANS):
         loads.append(pltpu.make_async_copy(table_hbm.at[j], table.at[j], load_sem.at[4 + j]))
+    loads.append(pltpu.make_async_copy(old_hbm.at[:, COLS:], old.at[:, COLS:], load_sem.at[6]))
     mat_loads = [
         pltpu.make_async_copy(
             mat_hbm.at[pl.ds(i * BLOCK, BLOCK)],
@@ -143,11 +150,22 @@
         )
         for i in range(NODES // BLOCK)
     ]
+    small = [
+        pltpu.make_async_copy(*pair, small_sem.at[i])
+        for i, pair in enumerate(
+            (
+                (nodes_hbm, nodes_ref),
+                (admit_hbm, admit_ref),
+                (hist_hbm, hist_ref),
+                (self_hbm, self_ref),
+                (region_hbm, region_ref),
+            )
+        )
+    ]
+    for load in small:
+        load.start()
     loads[0].start()
-    for load in mat_loads:
-        load.start()
-    for i in (2, 3, 4, 1, 5):
-        loads[i].start()
+    mat_loads[0].start()
 
     z_at, y_at, x_at, core_at = region // 16, region // 4 % 4, region // 2 % 2, region % 2
     z_part = [(z_at + i) % 4 * 16 for i in range(4)]
@@ -160,6 +178,15 @@
             barrier, inc=1, device_id={"region": peer, "sub": sub}, device_id_type=MESH
         )
     pl.semaphore_signal(barrier, inc=1, device_id=other_sub, device_id_type=MESH)
+
+    for load in small:
+        load.wait()
+    for i in (4, 2, 3):
+        loads[i].start()
+    for load in mat_loads[1:]:
+        load.start()
+    for i in (1, 6, 5):
+        loads[i].start()
 
     node_row = jnp.full((1, LANES), -1, jnp.int32)
     node_col = jnp.full((SLOTS, 1), -1, jnp.int32)
@@ -246,13 +273,13 @@
 
     def line_copies(j):
         copies = []
-        for at, count, to, device in ((0, 2, 0, other_sub), (2, 1, 3, below), (3, 1, 2, above)):
+        for at, to, device in ((sub, sub, other_sub), (2, 3, below), (3, 2, above)):
             copies.append(
                 pltpu.make_async_remote_copy(
-                    outgo.at[j, pl.ds(at, count)],
-                    arrived.at[j, pl.ds(to, count)],
-                    line_send.at[j, at],
-                    line_recv.at[j, to],
+                    outgo.at[j, at],
+                    arrived.at[j, to],
+                    line_send.at[j, len(copies)],
+                    line_recv.at[j, len(copies)],
                     device_id=device,
                     device_id_type=MESH,
                 )
@@ -284,6 +311,14 @@
     volts = part[:, PAD:] + term_gain * rhs[head, span0].astype(F32)
     fresh[0] = volts + dot(reach_parts, stack4(injected, injected))
 
+    for load in loads[2:5]:
+        load.wait()
+    base = jnp.concatenate([prior[pl.ds(0, TERM, stride=2), :], prior[pl.ds(1, TERM, stride=2), :]], axis=1)
+    fit = base + spectrum(fresh[0] - old[:, :COLS].astype(F32), 0)
+    post(0, pack(fit))
+
+    for j in range(SPANS):
+        arrived[j, sub] = jnp.zeros((LPP, COLS), F32)
     lax.fori_loop(1, NODES // BLOCK, weigh, 0)
     chosen = jnp.where(node_col == iota((SLOTS, NODES), 1), 1.0, 0.0)
     line_gain = jnp.sum(chosen * self_ref[...], axis=1, keepdims=True)
@@ -312,23 +347,40 @@
     for copy in lines0:
         copy.start()
 
-    for load in loads[2:5]:
-        load.wait()
-    base = jnp.concatenate([prior[pl.ds(0, TERM, stride=2), :], prior[pl.ds(1, TERM, stride=2), :]], axis=1)
-    fit = base + spectrum(fresh[0] - old[:, :COLS].astype(F32), 0)
-    post(0, pack(fit))
     send_items(0, peers)
     own_copy(0).start()
     volt_ref[head, pl.ds(0, COLS)] = fresh[0].astype(BF16)
 
     loads[1].wait()
     loads[5].wait()
+    loads[6].wait()
     part = dot(mat[: 2 * SLOTS + TERM, :], rhs[:, span1])
     line_base = part[:SLOTS] + line_gain * part[SLOTS : 2 * SLOTS]
     fresh[1] = part[2 * SLOTS :] + term_gain * rhs[head, span1].astype(F32)
     fit = fit + spectrum(fresh[1] - old[:, COLS:].astype(F32), 1)
     post(1, pack(fit))
     reach_box = dot(place, reach_parts).astype(BF16)
+
+    def inject(j, rows32):
+        injection = stack4(rows32)
+        columns = pl.ds(PAD + j * COLS, COLS)
+
+        def step(i, _):
+            rows = pl.ds(pl.multiple_of(i * FILL, FILL), FILL)
+            added = dot(rhs[rows, pl.ds(0, PAD)], injection)
+            rhs[rows, columns] = (rhs[rows, columns].astype(F32) + added).astype(BF16)
+            return 0
+
+        lax.fori_loop(0, NODES // FILL, step, 0)
+
+    def advance(i, _):
+        rows = pl.ds(pl.multiple_of(i * BLOCK, BLOCK), BLOCK)
+        total = dot(mat[pl.ds(2 * SLOTS + i * BLOCK, BLOCK), :], rhs[:, pl.ds(PAD, WIDE)])
+        total = total + gain[rows, :][:, :1] * rhs[rows, pl.ds(PAD, WIDE)].astype(F32)
+        volt_ref[rows, :] = total.astype(BF16)
+        return 0
+
+    inject(0, injected)
 
     for copy in lines0:
         copy.wait()
@@ -347,24 +399,7 @@
     for copy in lines1:
         copy.start()
 
-    injection = stack4(jnp.concatenate([injected, late], axis=1))
-
-    def inject(i, _):
-        rows = pl.ds(pl.multiple_of(i * FILL, FILL), FILL)
-        columns = pl.ds(PAD, WIDE)
-        added = dot(rhs[rows, pl.ds(0, PAD)], injection)
-        rhs[rows, columns] = (rhs[rows, columns].astype(F32) + added).astype(BF16)
-        return 0
-
-    lax.fori_loop(0, NODES // FILL, inject, 0)
-
-    def advance(i, _):
-        rows = pl.ds(pl.multiple_of(i * BLOCK, BLOCK), BLOCK)
-        total = dot(mat[pl.ds(2 * SLOTS + i * BLOCK, BLOCK), :], rhs[:, pl.ds(PAD, WIDE)])
-        total = total + gain[rows, :][:, :1] * rhs[rows, pl.ds(PAD, WIDE)].astype(F32)
-        volt_ref[rows, :] = total.astype(BF16)
-        return 0
-
+    inject(1, late)
     lax.fori_loop(1, NODES // BLOCK - LATE, advance, 0)
 
     for copy in lines1:
@@ -425,11 +460,10 @@
     any_space = pl.BlockSpec(memory_space=pl.ANY)
     hbm = pl.BlockSpec(memory_space=pltpu.HBM)
     vmem = pl.BlockSpec(memory_space=pltpu.VMEM)
-    smem = pl.BlockSpec(memory_space=pltpu.SMEM)
     held = pl.pallas_call(
         kernel,
         out_shape=tuple(pltpu.VMEM(shape, dtype) for shape, dtype in HELD),
-        in_specs=[smem, smem] + [hbm] * 5 + [vmem] * 3,
+        in_specs=[hbm] * 10,
         out_specs=(vmem,) * len(HELD),
         scratch_shapes=[
             pltpu.VMEM((TERM, WIDE), BF16),
@@ -440,12 +474,18 @@
             pltpu.VMEM((SPANS, NEIGH, LPP, COLS), F32),
             pltpu.VMEM((SPANS, 2, BOX, HARM), F32),
             pltpu.SemaphoreType.DMA((NODES // BLOCK,)),
-            pltpu.SemaphoreType.DMA((6,)),
-            pltpu.SemaphoreType.DMA((SPANS, NEIGH)),
-            pltpu.SemaphoreType.DMA((SPANS, NEIGH)),
+            pltpu.SemaphoreType.DMA((7,)),
+            pltpu.SemaphoreType.DMA((SPANS, 3)),
+            pltpu.SemaphoreType.DMA((SPANS, 3)),
             pltpu.SemaphoreType.DMA((SPANS,)),
             pltpu.SemaphoreType.DMA((SPANS,)),
             pltpu.SemaphoreType.DMA((SPANS,)),
+            pltpu.SMEM((NEIGH, LPP), jnp.int32),
+            pltpu.SMEM((NEIGH, LPP), F32),
+            pltpu.VMEM((SLOTS, COLS), F32),
+            pltpu.VMEM((1, NODES), F32),
+            pltpu.VMEM((1, TERM), jnp.int32),
+            pltpu.SemaphoreType.DMA((5,)),
         ],
         compiler_params=pltpu.CompilerParams(
             collective_id=0, has_side_effects=True, vmem_limit_bytes=38 << 20

time: 34.6 us -> 32.6 us (0.942)
  Pallas kernels: 33.8 us -> 31.8 us
    pallas_call x1, Pallas kernels: 31 us -> 29 us  [body(): pl.pallas_call(kernel, out_shape=tuple((pltpu.VMEM(shape, dtype) for shap...]
where the time goes in v3:
time: 32.6 us; the launch traced here: 32.4 us
  Pallas kernels  31.8 us (98%)
  between operations  0.64 us (2%)
    pallas_call x1, Pallas kernels, body(): pl.pallas_call(kernel, out_shape=tuple((pltpu.VMEM(shape, dtype) for shap...  29 us
    pallas_call x1, Pallas kernels, body(): pl.pallas_call(release, out_shape=tuple((jax.ShapeDtypeStruct(shape, dtyp...  2.85 us

profile of v3, /device:TPU:0, one launch (start us, length us, event | category | flops | bytes accessed | tf_op | source)
XLA Modules:
  0.0 32.4 jit_solution(8376212276456467898)
XLA Ops:
  0.6 29.0 %transient.1 = (bf16[2048,1280]{1,0:T(8,128)(2,1)S(1)}, f32[2,2,512,128]{3,2,1,0:T(8,128)S(1)}, f32[2,4,8,640]{3,2,1,0:T(8,128)S(1)}, bf16[2112,2048]{1,0:T(8,12...) custom-call(s32[4,8]{1,0:T(4,128)} %bitcast.14, f32[4,8]{1,0:T(4,128)} %bitcast.15, ...), custom_call_target="tpu_custom_call" | custom-call | tf_op jit(solution)/shard_map/transient/pallas_call | solution.py:463
  29.6 2.8 %release.1 = (bf16[2048,1280]{1,0:T(8,128)(2,1)}, f32[2048,128]{1,0:T(8,128)}, f32[4,8,640]{2,1,0:T(8,128)}) custom-call(bf16[2048,1280]{1,0:T(8,128)(2,1)S(1)} %get-tuple-element.12.volt_ref, f32[2,2,512,128]{3,2,1,0:T(8,128)S(1)} %get-tuple-element.13.landed, f32[2,4,8,640]{3,2,1,0:T(8,128)S(1)} %get-tuple-element.14.arrived, ...), custom_call_target="tpu_custom_call" | custom-call | tf_op jit(solution)/shard_map/release/pallas_call | solution.py:506
